TPU v7x, 256 devices: a whole 4x4x8 slice. The times are simulated.
256 devices in a mesh: dp: 32 (over x, z), section: 8 (over y, core).
Axes of the slice: x: 4, y: 4, z: 8, core: 2. Of those that a mesh axis runs over, the one named last changes fastest.
Arguments:
- tap_maps: bfloat16 [4, 2, 4096, 3200], P(None, None, ('dp', 'section')), may hold values from -6 to 6
- lateral_weight: bfloat16 [8, 3200, 768], P('section', 'dp'), may hold values from -0.109375 to 0.109375
- conv_weight: bfloat16 [8, 6912, 768], P('section'), may hold values from -0.078125 to 0.078125
- classifier: bfloat16 [768, 150], replicated, may hold values from -0.875 to 0.875
- tile_counts: int32 [32, 2], P('dp'), may hold values from 1 to 2, as said below
- labels: int32 [2, 4096], P(None, 'dp'), may hold values from 0 to 149
Outputs:
- conv_grad: float32 [8, 6912, 768], P('section', 'dp')
- lateral_grad: float32 [8, 3200, 768], P('section', 'dp')
Inputs may be any that keep to these rules, and one draw needn't show every extreme that they name: `tile_counts`: some entry equals 2.
All inputs are finite; a program needn't handle non-finite values.
Results may differ from a plain program's by a relative error of at most 0.035.
Values may be sent and summed in bfloat16 or wider, within the bound.
A program may use at most 128 MiB of HBM per device.

v0:
```python
import jax
import jax.numpy as jnp
from jax import lax
from jax.sharding import PartitionSpec as P

TILE_CAP = 2
BAND_ROWS = 1
BAND_COLS = 64


def padded_2(shard, sides, width):
    for axis, dim in sides:
        size, length = (lax.axis_size(axis), shard.shape[dim])
        up = [(i, (i + 1) % size) for i in range(size - 1)]
        down = [(j, i) for i, j in up]
        last = lax.slice_in_dim(shard, length - width, length, axis=dim)
        initial = lax.slice_in_dim(shard, 0, width, axis=dim)
        before = lax.ppermute(last, axis, up)
        after = lax.ppermute(initial, axis, down)
        shard = jnp.concatenate([before, shard, after], axis=dim)
    return shard


def shifted(block, axis, distance):
    devices = range(lax.axis_size(axis))
    route = [(i - distance, i) for i in devices if i - distance in devices]
    return lax.ppermute(block, axis, route)


def neighbour_shifts():
    return [(row_shift, col_shift) for row_shift in (-1, 0, 1) for col_shift in (-1, 0, 1)]


def widen(summed):
    grid = summed.reshape(TILE_CAP, BAND_ROWS, BAND_COLS, summed.shape[-1])
    return padded_2(grid, (("dp", 1),), 1)


def gather_columns(widened):
    chans = widened.shape[-1]
    padded = jnp.pad(widened, ((0, 0), (0, 0), (1, 1), (0, 0)))
    pieces = [
        padded[:, 1 + rs : 1 + rs + BAND_ROWS, 1 + cs : 1 + cs + BAND_COLS, :]
        for rs, cs in neighbour_shifts()
    ]
    return jnp.concatenate(pieces, axis=-1).reshape(-1, 9 * chans)


def spread_columns(grad_cols):
    chans = grad_cols.shape[-1] // 9
    grid = grad_cols.reshape(TILE_CAP, BAND_ROWS, BAND_COLS, 9, chans)
    total = jnp.zeros((TILE_CAP, BAND_ROWS + 2, BAND_COLS + 2, chans), jnp.float32)
    for offset, (rs, cs) in enumerate(neighbour_shifts()):
        total = total + jnp.pad(
            grid[:, :, :, offset, :], ((0, 0), (1 + rs, 1 - rs), (1 + cs, 1 - cs), (0, 0))
        )
    inner = total[:, 1:-1, 1:-1, :]
    rims = jnp.stack([total[:, 0, 1:-1, :], total[:, BAND_ROWS + 1, 1:-1, :]], axis=1)
    return (inner, rims)


def on_device(tap_maps, lateral_weight, conv_weight, classifier, tile_counts, labels):
    sections = lax.axis_size("section")
    groups = lax.axis_size("dp")
    place = lax.axis_index("section")
    levels = tap_maps.shape[0]
    micros = tap_maps.shape[1]
    width = tap_maps.shape[3]
    pixels = labels.shape[1]
    chans = conv_weight.shape[2]
    classes = classifier.shape[1]
    gathered = lax.all_gather(tap_maps, "section", axis=2, tiled=True)
    routed = lax.dynamic_index_in_dim(gathered, place * levels // sections, 0, keepdims=False)
    tap_rows = routed.reshape(micros * pixels, width)
    left = tap_rows
    lateral = jnp.dot(
        left,
        lax.all_gather(lateral_weight[0], "dp", axis=0, tiled=True),
        preferred_element_type=jnp.float32,
    )
    lateral = lateral.reshape(micros, pixels, chans)
    weights = conv_weight[0]
    ticks = sections + micros - 1

    def forward(step_count, carry):
        outgoing, widened_store, preact_store = carry
        incoming = shifted(outgoing, "section", 1)
        micro = step_count - place
        active = jnp.logical_and(micro >= 0, micro < micros)
        which = jnp.clip(micro, 0, micros - 1)
        summed = (
            incoming.astype(jnp.float32)
            + lax.dynamic_index_in_dim(lateral, which, 0, keepdims=False)
        ).astype(jnp.bfloat16)
        widened = widen(summed)

        def forward_advance(operands):
            extended, widened_old, preact_old = operands
            preact = jnp.dot(gather_columns(extended), weights, preferred_element_type=jnp.float32)
            activated = jax.nn.silu(preact).astype(jnp.bfloat16)
            return (
                activated,
                lax.dynamic_update_index_in_dim(widened_old, extended, which, 0),
                lax.dynamic_update_index_in_dim(preact_old, preact, which, 0),
            )

        def forward_skipped(operands):
            return (jnp.zeros((pixels, chans), jnp.bfloat16), operands[1], operands[2])

        return lax.cond(
            active, forward_advance, forward_skipped, (widened, widened_store, preact_store)
        )

    start_state = (
        jnp.zeros((pixels, chans), jnp.bfloat16),
        jnp.zeros((micros, TILE_CAP, BAND_ROWS + 2, BAND_COLS, chans), jnp.bfloat16),
        jnp.zeros((micros, pixels, chans), jnp.float32),
    )
    _, widened_store, preact_store = lax.fori_loop(0, ticks, forward, start_state)
    band = BAND_ROWS * BAND_COLS
    slot_ids = jnp.arange(pixels) // band
    per_count = tile_counts[0][:, None]
    valid = (slot_ids[None, :] < per_count).astype(jnp.float32)
    pixel_weight = valid / (per_count.astype(jnp.float32) * band * groups * micros)
    is_last = place == sections - 1
    class_ids = jnp.arange(classes)

    def backward(step_count, carry):
        outgoing, grad_pre_store, grad_in_store = carry
        incoming = shifted(outgoing, "section", -1)
        micro = step_count - (sections - 1 - place)
        active = jnp.logical_and(micro >= 0, micro < micros)
        which = jnp.clip(micro, 0, micros - 1)

        def backward_advance(operands):
            arrived, grad_pre_old = operands
            preact = lax.dynamic_index_in_dim(preact_store, which, 0, keepdims=False)
            activated = jax.nn.silu(preact).astype(jnp.bfloat16)
            logits = jnp.dot(activated, classifier, preferred_element_type=jnp.float32)
            expo = jnp.exp(logits)
            probs = expo / jnp.sum(expo, axis=-1, keepdims=True)
            label_row = lax.dynamic_index_in_dim(labels, which, 0, keepdims=False)
            onehot = (label_row[:, None] == class_ids[None, :]).astype(jnp.float32)
            weight_row = lax.dynamic_index_in_dim(pixel_weight, which, 0, keepdims=False)
            grad_logits = ((probs - onehot) * weight_row[:, None]).astype(jnp.bfloat16)
            from_loss = lax.dot_general(
                grad_logits,
                classifier,
                (((1,), (1,)), ((), ())),
                preferred_element_type=jnp.float32,
            )
            grad_out = jnp.where(is_last, from_loss, arrived.astype(jnp.float32))
            sigma = jax.nn.sigmoid(preact)
            grad_pre = (grad_out * sigma * (1.0 + preact * (1.0 - sigma))).astype(jnp.bfloat16)
            grad_cols = lax.dot_general(
                grad_pre, weights, (((1,), (1,)), ((), ())), preferred_element_type=jnp.float32
            )
            inner, rims = spread_columns(grad_cols)
            return (inner, rims, lax.dynamic_update_index_in_dim(grad_pre_old, grad_pre, which, 0))

        def backward_skipped(operands):
            return (
                jnp.zeros((TILE_CAP, BAND_ROWS, BAND_COLS, chans), jnp.float32),
                jnp.zeros((TILE_CAP, 2, BAND_COLS, chans), jnp.float32),
                operands[1],
            )

        inner, rims, grad_pre_store = lax.cond(
            active, backward_advance, backward_skipped, (incoming, grad_pre_store)
        )
        received = padded_2(rims.astype(jnp.bfloat16), (("dp", 1),), 1).astype(rims.dtype)
        inner = inner.at[:, 0].add(received[:, 0])
        inner = inner.at[:, BAND_ROWS - 1].add(received[:, 3])
        grad_in = inner.reshape(pixels, chans).astype(jnp.bfloat16)
        updated = lax.dynamic_update_index_in_dim(grad_in_store, grad_in, which, 0)
        grad_in_store = jnp.where(active, updated, grad_in_store)
        return (grad_in, grad_pre_store, grad_in_store)

    back_state = (
        jnp.zeros((pixels, chans), jnp.bfloat16),
        jnp.zeros((micros, pixels, chans), jnp.bfloat16),
        jnp.zeros((micros, pixels, chans), jnp.bfloat16),
    )
    _, grad_pre_store, grad_in_store = lax.fori_loop(0, ticks, backward, back_state)
    grad_pre_rows = grad_pre_store.reshape(micros * pixels, chans)
    grad_in_rows = grad_in_store.reshape(micros * pixels, chans)
    column_rows = gather_columns(
        widened_store.reshape(micros * TILE_CAP, BAND_ROWS + 2, BAND_COLS, chans)
    )
    left = tap_rows
    lateral_grad = lax.psum_scatter(
        lax.dot_general(
            left, grad_in_rows, (((0,), (0,)), ((), ())), preferred_element_type=jnp.float32
        ).astype(jnp.bfloat16),
        "dp",
        scatter_dimension=0,
        tiled=True,
    ).astype(jnp.float32)
    left = column_rows
    conv_grad = lax.psum_scatter(
        lax.dot_general(
            left, grad_pre_rows, (((0,), (0,)), ((), ())), preferred_element_type=jnp.float32
        ).astype(jnp.bfloat16),
        "dp",
        scatter_dimension=0,
        tiled=True,
    ).astype(jnp.float32)
    return (conv_grad[None], lateral_grad[None])


def solution(mesh):
    placed = (
        P(None, None, ("dp", "section"), None),
        P("section", "dp", None),
        P("section", None, None),
        P(),
        P("dp", None),
        P(None, "dp"),
    )
    return jax.shard_map(
        on_device,
        mesh=mesh,
        in_specs=placed,
        out_specs=(P("section", "dp", None), P("section", "dp", None)),
        check_vma=False,
    )
```

profile of v0, /device:TPU:8, one launch (start us, length us, event | category | flops | bytes accessed | tf_op | source)
XLA Modules:
  0.0 1171.2 jit_solution(1554315526162453511)
XLA Ops:
  10.9 45.6 %all-gather.4.cloned.1.call-done = bf16[4,2,128,3200]{3,2,1,0:T(8,128)(2,1)} async-done(((bf16[4,2,16,3200]{3,2,1,0:T(8,128)(2,1)}), bf16[4,2,128,3200]{3,2,1,0:T(8,128)(2,1)}) %all-gather.4.cloned.1.call-update) | async-done | bytes 6553616 | tf_op jit(solution)/shard_map/all_gather | solution.py:72
  58.0 108.3 %all-gather.6.cloned.1.call-done = bf16[1,3200,768]{2,0,1:T(2,128)(2,1)} async-done(((bf16[1,100,768]{2,0,1:T(2,128)(2,1)}), bf16[1,3200,768]{2,0,1:T(2,128)(2,1)}) %all-gather.6.cloned.1.call-update) | async-done | bytes 4915216 | tf_op jit(solution)/shard_map/all_gather | solution.py:78
  173.3 192.2 %while.43 = (s32[]{:T(128)}, bf16[128,768]{1,0:T(8,128)(2,1)}, bf16[2,2,3,64,768]{4,3,2,1,0:T(8,128)(2,1)S(1)}, f32[2,128,768]{2,1,0:T(8,128)}, s32[]{:T(128)}, ...) while((s32[]{:T(128)}, bf16[128,768]{1,0:T(8,128)(2,1)}, ...), condition=%wide.region_3.4_spmd, body=%wide.region_0.3_spmd.sunk | while | flops 1360330752 | bytes 25166232 | solution.py:119
  212.7 9.7 collective-permute-done
  234.0 7.6 conditional.5
  234.5 6.3 multiply_convert_fusion
  260.3 7.6 conditional.5
  260.7 6.3 multiply_convert_fusion
  325.8 6.5 collective-permute-start
  369.7 504.1 %while.44 = (s32[]{:T(128)}, bf16[128,768]{1,0:T(8,128)(2,1)S(1)}, bf16[2,128,768]{2,1,0:T(8,128)(2,1)}, bf16[2,128,768]{2,1,0:T(8,128)(2,1)}, s32[]{:T(128)}, /...) while((s32[]{:T(128)}, bf16[128,768]{1,0:T(8,128)(2,1)S(1)}, ...), condition=%wide.region_8.9_spmd.clone, body=%wide.region_4.8_spmd.clone.sunk | while | flops 1424437120 | bytes 46599908 | solution.py:184
  454.4 6.9 collective-permute-done.3
  511.5 161.1 %collective-permute-done.3 = bf16[128,768]{1,0:T(8,128)(2,1)S(1)} collective-permute-done((bf16[128,768]{1,0:T(8,128)(2,1)S(1)}, bf16[128,768]{1,0:T(8,128)(2,1)S(1)}, u32[]{:S(2)}, u32[]{:S(2)}) %collective-permute-start.3) | collective-permute-done | bytes 196640 | tf_op jit(solution)/shard_map/while/body/eval_jaxpr/ppermute | solution.py:27
  672.6 34.2 %conditional.6 = (f32[2,1,64,768]{3,1,2,0:T(1,128)}, bf16[2,2,64,768]{3,1,2,0:T(2,128)(2,1)}, bf16[2,128,768]{2,1,0:T(8,128)(2,1)}) conditional(s32[]{:T(128)} %convert_element_type.205, bf16[2,128,768]{2,1,0:T(8,128)(2,1)} %get-tuple-element.928, (pred[]{:T(512)}, s32[]{:T(128)}, f32[2,128,768]{2,1,0:T(8,128)}, bf16[768,150]{1,0:T(8,128)(2,1)}, ...), branch_computations={%region_5.5_spmd, %region_6.7_spmd} | conditional | flops 1422863744 | bytes 37946536 | solution.py:168
  677.0 7.5 fusion.47
  687.8 12.8 %slice_bitcast_fusion.8 = (f32[2,1,64,768]{3,1,2,0:T(1,128)S(1)}, f32[2,1,64,768]{3,1,2,0:T(1,128)S(1)}, f32[2,1,64,768]{3,1,2,0:T(1,128)S(1)}, f32[2,1,64,768]{...) fusion(f32[2,1,64,9,768]{4,3,2,0,1:T(8,128)} %reshape.209), kind=kLoop, calls=%fused_computation.38 | loop fusion | bytes 7077888 | tf_op jit(solution)/shard_map/while/body/eval_jaxpr/cond/branch_1_fun/squeeze | solution.py:55
  710.0 6.2 collective-permute-start.5
  733.4 34.2 %conditional.6 = (f32[2,1,64,768]{3,1,2,0:T(1,128)}, bf16[2,2,64,768]{3,1,2,0:T(2,128)(2,1)}, bf16[2,128,768]{2,1,0:T(8,128)(2,1)}) conditional(s32[]{:T(128)} %convert_element_type.205, bf16[2,128,768]{2,1,0:T(8,128)(2,1)} %get-tuple-element.928, (pred[]{:T(512)}, s32[]{:T(128)}, f32[2,128,768]{2,1,0:T(8,128)}, bf16[768,150]{1,0:T(8,128)(2,1)}, ...), branch_computations={%region_5.5_spmd, %region_6.7_spmd} | conditional | flops 1422863744 | bytes 37946536 | solution.py:168
  737.8 7.5 fusion.47
  748.5 12.8 %slice_bitcast_fusion.8 = (f32[2,1,64,768]{3,1,2,0:T(1,128)S(1)}, f32[2,1,64,768]{3,1,2,0:T(1,128)S(1)}, f32[2,1,64,768]{3,1,2,0:T(1,128)S(1)}, f32[2,1,64,768]{...) fusion(f32[2,1,64,9,768]{4,3,2,0,1:T(8,128)} %reshape.209), kind=kLoop, calls=%fused_computation.38 | loop fusion | bytes 7077888 | tf_op jit(solution)/shard_map/while/body/eval_jaxpr/cond/branch_1_fun/squeeze | solution.py:55
  796.9 6.3 collective-permute-start.5
  814.8 34.6 %collective-permute-start.3 = (bf16[128,768]{1,0:T(8,128)(2,1)S(1)}, bf16[128,768]{1,0:T(8,128)(2,1)S(1)}, u32[]{:S(2)}, u32[]{:S(2)}) collective-permute-start(bf16[128,768]{1,0:T(8,128)(2,1)S(1)} %get-tuple-element.927), channel_id=1, source_target_pairs={{1,0},{2,1},{3,2},{4,3},{5,4},{6,5},{7,6},{9,8},{10,9},{11,10},{12... | collective-permute-start | bytes 589832 | tf_op jit(solution)/shard_map/while/body/eval_jaxpr/ppermute | solution.py:27
  873.8 9.1 convolution_convert_fusion
  888.2 111.0 %fusion.4 = bf16[104,768]{1,0:T(8,128)(2,1)S(1)} fusion(bf16[3200,768]{1,0:T(8,128)(2,1)} %convolution_convert_fusion.1), kind=kCustom, calls=%all-reduce-scatter | all-reduce-scatter fusion | flops 2555905 | bytes 5075968
  1007.1 155.7 %reduce-scatter.4.cloned.1.call-done = bf16[216,768]{1,0:T(8,128)(2,1)} async-done(((bf16[6912,768]{1,0:T(8,128)(2,1)}), bf16[216,768]{1,0:T(8,128)(2,1)}) %reduce-scatter.4.cloned.1.call-update) | async-done | bytes 331792 | tf_op jit(solution)/shard_map/reduce_scatter | solution.py:200
  (338 shorter events, 459.3 us)
Async XLA Ops:
  7.2 49.3 %all-gather.4.cloned.1.call-start = ((), (), s32[]{:S(2)}) async-start(), calls=%async_computation.1 | async-start | bytes 7372800 | tf_op jit(solution)/shard_map/all_gather | solution.py:72
  7.9 158.4 %all-gather.6.cloned.1.call-start = ((), (), s32[]{:S(2)}) async-start(), calls=%async_computation.3 | async-start | bytes 10137600 | tf_op jit(solution)/shard_map/all_gather | solution.py:78
  9.9 1152.9 %reduce-scatter.4.cloned.1.call-start = ((), (), s32[]{:S(2)}) async-start(), calls=%async_computation.2 | async-start | bytes 10948608 | tf_op jit(solution)/shard_map/reduce_scatter | solution.py:200
  210.8 11.6 collective-permute-start
  380.9 9.8 collective-permute-start.4
  382.2 9.9 collective-permute-start.5
  408.5 9.8 collective-permute-start.4
  409.8 10.0 collective-permute-start.5
  436.3 9.8 collective-permute-start.4
  437.6 10.0 collective-permute-start.5
  465.1 10.7 collective-permute-start.4
  466.4 11.1 collective-permute-start.5
  492.3 11.1 collective-permute-start.4
  493.6 11.2 collective-permute-start.5
  509.5 163.1 %collective-permute-start.3 = (bf16[128,768]{1,0:T(8,128)(2,1)S(1)}, bf16[128,768]{1,0:T(8,128)(2,1)S(1)}, u32[]{:S(2)}, u32[]{:S(2)}) collective-permute-start(bf16[128,768]{1,0:T(8,128)(2,1)S(1)} %get-tuple-element.927), channel_id=1, source_target_pairs={{1,0},{2,1},{3,2},{4,3},{5,4},{6,5},{7,6},{9,8},{10,9},{11,10},{12... | collective-permute-start | bytes 589832 | tf_op jit(solution)/shard_map/while/body/eval_jaxpr/ppermute | solution.py:27
  708.7 11.9 %collective-permute-start.4 = (bf16[2,1,64,768]{3,1,2,0:T(2,128)(2,1)S(1)}, bf16[2,1,64,768]{3,1,2,0:T(2,128)(2,1)S(1)}, u32[]{:S(2)}, u32[]{:S(2)}) collective-permute-start(bf16[2,1,64,768]{3,1,2,0:T(2,128)(2,1)S(1)} %get-tuple-element.864), channel_id=1, source_target_pairs={{8,0},{16,8},{24,16},{32,24},{40,32},{48,40},{56,48},{64,56},{72,6... | collective-permute-start | bytes 589832 | tf_op jit(solution)/shard_map/while/body/eval_jaxpr/ppermute | solution.py:19
  710.0 12.4 %collective-permute-start.5 = (bf16[2,1,64,768]{3,1,2,0:T(2,128)(2,1)S(1)}, bf16[2,1,64,768]{3,1,2,0:T(2,128)(2,1)S(1)}, u32[]{:S(2)}, u32[]{:S(2)}) collective-permute-start(bf16[2,1,64,768]{3,1,2,0:T(2,128)(2,1)S(1)} %get-tuple-element.865), channel_id=1, source_target_pairs={{0,8},{8,16},{16,24},{24,32},{32,40},{40,48},{48,56},{56,64},{64,7... | collective-permute-start | bytes 589832 | tf_op jit(solution)/shard_map/while/body/eval_jaxpr/ppermute | solution.py:18
  769.4 11.0 collective-permute-start.4
  770.7 11.2 collective-permute-start.5
  795.6 13.3 %collective-permute-start.4 = (bf16[2,1,64,768]{3,1,2,0:T(2,128)(2,1)S(1)}, bf16[2,1,64,768]{3,1,2,0:T(2,128)(2,1)S(1)}, u32[]{:S(2)}, u32[]{:S(2)}) collective-permute-start(bf16[2,1,64,768]{3,1,2,0:T(2,128)(2,1)S(1)} %get-tuple-element.864), channel_id=1, source_target_pairs={{8,0},{16,8},{24,16},{32,24},{40,32},{48,40},{56,48},{64,56},{72,6... | collective-permute-start | bytes 589832 | tf_op jit(solution)/shard_map/while/body/eval_jaxpr/ppermute | solution.py:19
  796.9 13.2 %collective-permute-start.5 = (bf16[2,1,64,768]{3,1,2,0:T(2,128)(2,1)S(1)}, bf16[2,1,64,768]{3,1,2,0:T(2,128)(2,1)S(1)}, u32[]{:S(2)}, u32[]{:S(2)}) collective-permute-start(bf16[2,1,64,768]{3,1,2,0:T(2,128)(2,1)S(1)} %get-tuple-element.865), channel_id=1, source_target_pairs={{0,8},{8,16},{16,24},{24,32},{32,40},{40,48},{48,56},{56,64},{64,7... | collective-permute-start | bytes 589832 | tf_op jit(solution)/shard_map/while/body/eval_jaxpr/ppermute | solution.py:18
  814.8 37.7 %collective-permute-start.3 = (bf16[128,768]{1,0:T(8,128)(2,1)S(1)}, bf16[128,768]{1,0:T(8,128)(2,1)S(1)}, u32[]{:S(2)}, u32[]{:S(2)}) collective-permute-start(bf16[128,768]{1,0:T(8,128)(2,1)S(1)} %get-tuple-element.927), channel_id=1, source_target_pairs={{1,0},{2,1},{3,2},{4,3},{5,4},{6,5},{7,6},{9,8},{10,9},{11,10},{12... | collective-permute-start | bytes 589832 | tf_op jit(solution)/shard_map/while/body/eval_jaxpr/ppermute | solution.py:27
  856.3 12.7 %collective-permute-start.4 = (bf16[2,1,64,768]{3,1,2,0:T(2,128)(2,1)S(1)}, bf16[2,1,64,768]{3,1,2,0:T(2,128)(2,1)S(1)}, u32[]{:S(2)}, u32[]{:S(2)}) collective-permute-start(bf16[2,1,64,768]{3,1,2,0:T(2,128)(2,1)S(1)} %get-tuple-element.864), channel_id=1, source_target_pairs={{8,0},{16,8},{24,16},{32,24},{40,32},{48,40},{56,48},{64,56},{72,6... | collective-permute-start | bytes 589832 | tf_op jit(solution)/shard_map/while/body/eval_jaxpr/ppermute | solution.py:19
  857.6 11.4 collective-permute-start.5
  (60 other events, 659.9 us)
Sparse Core Ops, SparseCore 0:
  9.9 46.5 all-gather.3
  59.6 106.6 all-gather.5
  883.1 279.6 reduce-scatter.3
where the time goes:
time: 1170 us
  waiting for transfers between devices  663 us (57%)
  starting transfers between devices  185 us (16%)
  blocking collectives  111 us (9%)
  local copies, waits for them, and re-layouts  94.6 us (8%)
  matrix products  53 us (5%)
  other arithmetic  48.3 us (4%)
  between operations  14.6 us (1%)
    ppermute x18, waiting for transfers between devices, shifted(): return lax.ppermute(block, axis, route)  242 us
    reduce_scatter x1, waiting for transfers between devices, on_device(): lax.psum_scatter(lax.dot_general(left, grad_pre_rows, (((0,), (0,)), ((),...  156 us
    unnamed x1, blocking collectives  111 us
    all_gather x1, waiting for transfers between devices, on_device(): lax.all_gather(lateral_weight[0], 'dp', axis=0, tiled=True)  108 us
    ppermute x18, starting transfers between devices, padded_2(): before = lax.ppermute(last, axis, up)  82.1 us
    ppermute x18, waiting for transfers between devices, padded_2(): after = lax.ppermute(initial, axis, down)  78 us
    ppermute x18, starting transfers between devices, shifted(): return lax.ppermute(block, axis, route)  77.3 us
    all_gather x1, waiting for transfers between devices, on_device(): gathered = lax.all_gather(tap_maps, 'section', axis=2, tiled=True)  45.6 us
  transfers between devices with their start and end apart: 59, of which 57 were waited for; matrix products, arithmetic and copies ran while one was open for 10% of the time, Pallas kernels for 0%

commit v1 on v0

--- a/solution.py
+++ b/solution.py
@@ -69,7 +69,25 @@
     pixels = labels.shape[1]
     chans = conv_weight.shape[2]
     classes = classifier.shape[1]
-    gathered = lax.all_gather(tap_maps, "section", axis=2, tiled=True)
+    clean, even, view_out = (lax.axis_size("section"), lax.axis_index("section"), tap_maps.shape[2])
+    inbox = [(w, (w + 1) % clean) for w in range(clean)]
+    pages = [(w, (w - 1) % clean) for w in range(clean)]
+    gathered = jnp.zeros(
+        (*tap_maps.shape[:2], clean * view_out, *tap_maps.shape[2 + 1 :]), tap_maps.dtype
+    )
+    gathered = lax.dynamic_update_slice_in_dim(gathered, tap_maps, even * view_out, axis=2)
+    upper = y2 = tap_maps
+    arr_now = clean // 2
+    for d in range(1, arr_now + 1):
+        upper = lax.ppermute(upper, "section", inbox)
+        gathered = lax.dynamic_update_slice_in_dim(
+            gathered, upper, (even - d) % clean * view_out, axis=2
+        )
+        if d < clean - arr_now:
+            y2 = lax.ppermute(y2, "section", pages)
+            gathered = lax.dynamic_update_slice_in_dim(
+                gathered, y2, (even + d) % clean * view_out, axis=2
+            )
     routed = lax.dynamic_index_in_dim(gathered, place * levels // sections, 0, keepdims=False)
     tap_rows = routed.reshape(micros * pixels, width)
     left = tap_rows

time: 1170 us -> 1120 us (0.957)
  waiting for transfers between devices: 663 us -> 579 us
  starting transfers between devices: 185 us -> 214 us
    all_gather x1 -> x0, waiting for transfers between devices: 45.6 us -> none  [on_device(): gathered = lax.all_gather(tap_maps, 'section', axis=2, tiled=True)]
    all_gather x1, waiting for transfers between devices: 108 us -> 63 us  [on_device(): lax.all_gather(lateral_weight[0], 'dp', axis=0, tiled=True)]
    ppermute x0 -> x7, waiting for transfers between devices: none -> 36.9 us  [the longest x4 36.3 us: on_device(): upper = lax.ppermute(upper, 'section', inbox)]
    ppermute x18, waiting for transfers between devices: 78 us -> 55.9 us  [padded_2(): after = lax.ppermute(initial, axis, down)]
    ppermute x18, starting transfers between devices: 82.1 us -> 103 us  [padded_2(): before = lax.ppermute(last, axis, up)]
  transfers between devices with their start and end apart: 59 -> 65, of which waited for: 57 -> 63; matrix products, arithmetic and copies ran while one was open for 10% -> 11% of each run, Pallas kernels for 0% -> 0%
where the time goes in v1:
time: 1120 us
  waiting for transfers between devices  579 us (52%)
  starting transfers between devices  214 us (19%)
  blocking collectives  114 us (10%)
  local copies, waits for them, and re-layouts  95.2 us (8%)
  matrix products  53 us (5%)
  other arithmetic  48.9 us (4%)
  between operations  15 us (1%)
    ppermute x18, waiting for transfers between devices, shifted(): return lax.ppermute(block, axis, route)  241 us
    reduce_scatter x1, waiting for transfers between devices, on_device(): lax.psum_scatter(lax.dot_general(left, grad_pre_rows, (((0,), (0,)), ((),...  155 us
    unnamed x1, blocking collectives  114 us
    ppermute x18, starting transfers between devices, padded_2(): before = lax.ppermute(last, axis, up)  103 us
    ppermute x18, starting transfers between devices, shifted(): return lax.ppermute(block, axis, route)  78.2 us
    all_gather x1, waiting for transfers between devices, on_device(): lax.all_gather(lateral_weight[0], 'dp', axis=0, tiled=True)  63 us
    ppermute x18, waiting for transfers between devices, padded_2(): after = lax.ppermute(initial, axis, down)  55.9 us
    ppermute x4, waiting for transfers between devices, on_device(): upper = lax.ppermute(upper, 'section', inbox)  36.3 us
  transfers between devices with their start and end apart: 65, of which 63 were waited for; matrix products, arithmetic and copies ran while one was open for 11% of the time, Pallas kernels for 0%

profile of v1, /device:TPU:8, one launch (start us, length us, event | category | flops | bytes accessed | tf_op | source)
XLA Modules:
  0.0 1120.7 jit_solution(14985662680587684647)
XLA Ops:
  14.5 6.7 collective-permute-done.6
  23.4 9.5 collective-permute-done.8
  35.6 9.1 collective-permute-done.10
  45.3 11.1 collective-permute-done.12
  56.7 63.0 %all-gather.3.cloned.1.call-done = bf16[1,3200,768]{2,0,1:T(2,128)(2,1)} async-done(((bf16[1,100,768]{2,0,1:T(2,128)(2,1)}), bf16[1,3200,768]{2,0,1:T(2,128)(2,1)}) %all-gather.3.cloned.1.call-update) | async-done | bytes 4915216 | tf_op jit(solution)/shard_map/all_gather | solution.py:96
  126.8 181.3 %while.43 = (s32[]{:T(128)}, bf16[128,768]{1,0:T(8,128)(2,1)}, bf16[2,2,3,64,768]{4,3,2,1,0:T(8,128)(2,1)S(1)}, f32[2,128,768]{2,1,0:T(8,128)}, s32[]{:T(128)}, ...) while((s32[]{:T(128)}, bf16[128,768]{1,0:T(8,128)(2,1)}, ...), condition=%wide.region_3.4_spmd, body=%wide.region_0.3_spmd.sunk | while | flops 1360330752 | bytes 25166232 | solution.py:137
  163.6 10.1 collective-permute-done
  182.9 7.6 conditional.5
  183.4 6.3 multiply_convert_fusion
  207.3 7.5 conditional.5
  270.1 6.8 collective-permute-start
  311.6 508.9 %while.44 = (s32[]{:T(128)}, bf16[128,768]{1,0:T(8,128)(2,1)S(1)}, bf16[2,128,768]{2,1,0:T(8,128)(2,1)}, bf16[2,128,768]{2,1,0:T(8,128)(2,1)}, s32[]{:T(128)}, /...) while((s32[]{:T(128)}, bf16[128,768]{1,0:T(8,128)(2,1)S(1)}, ...), condition=%wide.region_8.9_spmd.clone, body=%wide.region_4.8_spmd.clone.sunk | while | flops 1424437120 | bytes 46599908 | solution.py:202
  400.9 6.6 collective-permute-done.3
  459.1 160.8 %collective-permute-done.3 = bf16[128,768]{1,0:T(8,128)(2,1)S(1)} collective-permute-done((bf16[128,768]{1,0:T(8,128)(2,1)S(1)}, bf16[128,768]{1,0:T(8,128)(2,1)S(1)}, u32[]{:S(2)}, u32[]{:S(2)}) %collective-permute-start.3) | collective-permute-done | bytes 196640 | tf_op jit(solution)/shard_map/while/body/eval_jaxpr/ppermute | solution.py:27
  619.8 34.1 %conditional.6 = (f32[2,1,64,768]{3,1,2,0:T(1,128)}, bf16[2,2,64,768]{3,1,2,0:T(2,128)(2,1)}, bf16[2,128,768]{2,1,0:T(8,128)(2,1)}) conditional(s32[]{:T(128)} %convert_element_type.205, bf16[2,128,768]{2,1,0:T(8,128)(2,1)} %get-tuple-element.928, (pred[]{:T(512)}, s32[]{:T(128)}, f32[2,128,768]{2,1,0:T(8,128)}, bf16[768,150]{1,0:T(8,128)(2,1)}, ...), branch_computations={%region_5.5_spmd, %region_6.7_spmd} | conditional | flops 1422863744 | bytes 37946536 | solution.py:186
  624.2 7.5 fusion.47
  635.0 12.7 %slice_bitcast_fusion.8 = (f32[2,1,64,768]{3,1,2,0:T(1,128)S(1)}, f32[2,1,64,768]{3,1,2,0:T(1,128)S(1)}, f32[2,1,64,768]{3,1,2,0:T(1,128)S(1)}, f32[2,1,64,768]{...) fusion(f32[2,1,64,9,768]{4,3,2,0,1:T(8,128)} %reshape.209), kind=kLoop, calls=%fused_computation.38 | loop fusion | bytes 7077888 | tf_op jit(solution)/shard_map/while/body/eval_jaxpr/cond/branch_1_fun/squeeze | solution.py:55
  680.5 34.1 %conditional.6 = (f32[2,1,64,768]{3,1,2,0:T(1,128)}, bf16[2,2,64,768]{3,1,2,0:T(2,128)(2,1)}, bf16[2,128,768]{2,1,0:T(8,128)(2,1)}) conditional(s32[]{:T(128)} %convert_element_type.205, bf16[2,128,768]{2,1,0:T(8,128)(2,1)} %get-tuple-element.928, (pred[]{:T(512)}, s32[]{:T(128)}, f32[2,128,768]{2,1,0:T(8,128)}, bf16[768,150]{1,0:T(8,128)(2,1)}, ...), branch_computations={%region_5.5_spmd, %region_6.7_spmd} | conditional | flops 1422863744 | bytes 37946536 | solution.py:186
  684.9 7.5 fusion.47
  695.6 12.7 %slice_bitcast_fusion.8 = (f32[2,1,64,768]{3,1,2,0:T(1,128)S(1)}, f32[2,1,64,768]{3,1,2,0:T(1,128)S(1)}, f32[2,1,64,768]{3,1,2,0:T(1,128)S(1)}, f32[2,1,64,768]{...) fusion(f32[2,1,64,9,768]{4,3,2,0,1:T(8,128)} %reshape.209), kind=kLoop, calls=%fused_computation.38 | loop fusion | bytes 7077888 | tf_op jit(solution)/shard_map/while/body/eval_jaxpr/cond/branch_1_fun/squeeze | solution.py:55
  761.8 34.5 %collective-permute-start.3 = (bf16[128,768]{1,0:T(8,128)(2,1)S(1)}, bf16[128,768]{1,0:T(8,128)(2,1)S(1)}, u32[]{:S(2)}, u32[]{:S(2)}) collective-permute-start(bf16[128,768]{1,0:T(8,128)(2,1)S(1)} %get-tuple-element.927), channel_id=1, source_target_pairs={{1,0},{2,1},{3,2},{4,3},{5,4},{6,5},{7,6},{9,8},{10,9},{11,10},{12... | collective-permute-start | bytes 589832 | tf_op jit(solution)/shard_map/while/body/eval_jaxpr/ppermute | solution.py:27
  820.5 9.1 convolution_convert_fusion
  834.8 113.7 %fusion.4 = bf16[104,768]{1,0:T(8,128)(2,1)S(1)} fusion(bf16[3200,768]{1,0:T(8,128)(2,1)} %convolution_convert_fusion.1), kind=kCustom, calls=%all-reduce-scatter | all-reduce-scatter fusion | flops 2555905 | bytes 5075968
  956.9 155.1 %reduce-scatter.4.cloned.1.call-done = bf16[216,768]{1,0:T(8,128)(2,1)} async-done(((bf16[6912,768]{1,0:T(8,128)(2,1)}), bf16[216,768]{1,0:T(8,128)(2,1)}) %reduce-scatter.4.cloned.1.call-update) | async-done | bytes 331792 | tf_op jit(solution)/shard_map/reduce_scatter | solution.py:218
  (358 shorter events, 479.6 us)
Async XLA Ops:
  7.2 112.6 %all-gather.3.cloned.1.call-start = ((), (), s32[]{:S(2)}) async-start(), calls=%async_computation.2 | async-start | bytes 10137600 | tf_op jit(solution)/shard_map/all_gather | solution.py:96
  9.1 1102.9 %reduce-scatter.4.cloned.1.call-start = ((), (), s32[]{:S(2)}) async-start(), calls=%async_computation.1 | async-start | bytes 10948608 | tf_op jit(solution)/shard_map/reduce_scatter | solution.py:218
  9.2 12.0 %collective-permute-start.6 = (bf16[4,2,16,3200]{3,2,1,0:T(8,128)(2,1)}, bf16[4,2,16,3200]{3,2,1,0:T(8,128)(2,1)S(1)}, u32[]{:S(2)}, u32[]{:S(2)}) collective-permute-start(bf16[4,2,16,3200]{3,2,1,0:T(8,128)(2,1)} %param.18), channel_id=1, source_target_pairs={{0,1},{1,2},{2,3},{3,4},{4,5},{5,6},{6,7},{7,0},{8,9},{9,10},{10,1... | collective-permute-start | bytes 2457608 | tf_op jit(solution)/shard_map/ppermute | solution.py:82
  9.2 12.0 %collective-permute-start.7 = (bf16[4,2,16,3200]{3,2,1,0:T(8,128)(2,1)}, bf16[4,2,16,3200]{3,2,1,0:T(8,128)(2,1)S(1)}, u32[]{:S(2)}, u32[]{:S(2)}) collective-permute-start(bf16[4,2,16,3200]{3,2,1,0:T(8,128)(2,1)} %param.18), channel_id=1, source_target_pairs={{0,7},{1,0},{2,1},{3,2},{4,3},{5,4},{6,5},{7,6},{8,15},{9,8},{10,9... | collective-permute-start | bytes 2457608 | tf_op jit(solution)/shard_map/ppermute | solution.py:87
  21.1 11.8 %collective-permute-start.8 = (bf16[4,2,16,3200]{3,2,1,0:T(8,128)(2,1)S(1)}, bf16[4,2,16,3200]{3,2,1,0:T(8,128)(2,1)S(1)}, u32[]{:S(2)}, u32[]{:S(2)}) collective-permute-start(bf16[4,2,16,3200]{3,2,1,0:T(8,128)(2,1)S(1)} %collective-permute-done.6), channel_id=1, source_target_pairs={{0,1},{1,2},{2,3},{3,4},{4,5},{5,6},{6,7},{7,0},{8,9},{9,10},{10,1... | collective-permute-start | bytes 2457608 | tf_op jit(solution)/shard_map/ppermute | solution.py:82
  21.1 11.9 %collective-permute-start.9 = (bf16[4,2,16,3200]{3,2,1,0:T(8,128)(2,1)S(1)}, bf16[4,2,16,3200]{3,2,1,0:T(8,128)(2,1)S(1)}, u32[]{:S(2)}, u32[]{:S(2)}) collective-permute-start(bf16[4,2,16,3200]{3,2,1,0:T(8,128)(2,1)S(1)} %collective-permute-done.7), channel_id=1, source_target_pairs={{0,7},{1,0},{2,1},{3,2},{4,3},{5,4},{6,5},{7,6},{8,15},{9,8},{10,9... | collective-permute-start | bytes 2457608 | tf_op jit(solution)/shard_map/ppermute | solution.py:87
  32.9 11.8 %collective-permute-start.10 = (bf16[4,2,16,3200]{3,2,1,0:T(8,128)(2,1)S(1)}, bf16[4,2,16,3200]{3,2,1,0:T(8,128)(2,1)S(1)}, u32[]{:S(2)}, u32[]{:S(2)}) collective-permute-start(bf16[4,2,16,3200]{3,2,1,0:T(8,128)(2,1)S(1)} %collective-permute-done.8), channel_id=1, source_target_pairs={{0,1},{1,2},{2,3},{3,4},{4,5},{5,6},{6,7},{7,0},{8,9},{9,10},{10,1... | collective-permute-start | bytes 2457608 | tf_op jit(solution)/shard_map/ppermute | solution.py:82
  33.0 12.2 %collective-permute-start.11 = (bf16[4,2,16,3200]{3,2,1,0:T(8,128)(2,1)S(1)}, bf16[4,2,16,3200]{3,2,1,0:T(8,128)(2,1)S(1)}, u32[]{:S(2)}, u32[]{:S(2)}) collective-permute-start(bf16[4,2,16,3200]{3,2,1,0:T(8,128)(2,1)S(1)} %collective-permute-done.9), channel_id=1, source_target_pairs={{0,7},{1,0},{2,1},{3,2},{4,3},{5,4},{6,5},{7,6},{8,15},{9,8},{10,9... | collective-permute-start | bytes 2457608 | tf_op jit(solution)/shard_map/ppermute | solution.py:87
  44.7 11.8 %collective-permute-start.12 = (bf16[4,2,16,3200]{3,2,1,0:T(8,128)(2,1)S(1)}, bf16[4,2,16,3200]{3,2,1,0:T(8,128)(2,1)S(1)}, u32[]{:S(2)}, u32[]{:S(2)}) collective-permute-start(bf16[4,2,16,3200]{3,2,1,0:T(8,128)(2,1)S(1)} %collective-permute-done.10), channel_id=1, source_target_pairs={{0,1},{1,2},{2,3},{3,4},{4,5},{5,6},{6,7},{7,0},{8,9},{9,10},{10,1... | collective-permute-start | bytes 2457608 | tf_op jit(solution)/shard_map/ppermute | solution.py:82
  161.7 12.0 %collective-permute-start = (bf16[128,768]{1,0:T(8,128)(2,1)}, bf16[128,768]{1,0:T(8,128)(2,1)S(1)}, u32[]{:S(2)}, u32[]{:S(2)}) collective-permute-start(bf16[128,768]{1,0:T(8,128)(2,1)} %get-tuple-element.891), channel_id=1, source_target_pairs={{0,1},{1,2},{2,3},{3,4},{4,5},{5,6},{6,7},{8,9},{9,10},{10,11},{11... | collective-permute-start | bytes 589832 | tf_op jit(solution)/shard_map/while/body/eval_jaxpr/ppermute | solution.py:27
  323.6 11.3 %collective-permute-start.4 = (bf16[2,1,64,768]{3,1,2,0:T(2,128)(2,1)S(1)}, bf16[2,1,64,768]{3,1,2,0:T(2,128)(2,1)S(1)}, u32[]{:S(2)}, u32[]{:S(2)}) collective-permute-start(bf16[2,1,64,768]{3,1,2,0:T(2,128)(2,1)S(1)} %get-tuple-element.864), channel_id=1, source_target_pairs={{8,0},{16,8},{24,16},{32,24},{40,32},{48,40},{56,48},{64,56},{72,6... | collective-permute-start | bytes 589832 | tf_op jit(solution)/shard_map/while/body/eval_jaxpr/ppermute | solution.py:19
  324.9 11.5 %collective-permute-start.5 = (bf16[2,1,64,768]{3,1,2,0:T(2,128)(2,1)S(1)}, bf16[2,1,64,768]{3,1,2,0:T(2,128)(2,1)S(1)}, u32[]{:S(2)}, u32[]{:S(2)}) collective-permute-start(bf16[2,1,64,768]{3,1,2,0:T(2,128)(2,1)S(1)} %get-tuple-element.865), channel_id=1, source_target_pairs={{0,8},{8,16},{16,24},{24,32},{32,40},{40,48},{48,56},{56,64},{64,7... | collective-permute-start | bytes 589832 | tf_op jit(solution)/shard_map/while/body/eval_jaxpr/ppermute | solution.py:18
  353.8 11.3 %collective-permute-start.5 = (bf16[2,1,64,768]{3,1,2,0:T(2,128)(2,1)S(1)}, bf16[2,1,64,768]{3,1,2,0:T(2,128)(2,1)S(1)}, u32[]{:S(2)}, u32[]{:S(2)}) collective-permute-start(bf16[2,1,64,768]{3,1,2,0:T(2,128)(2,1)S(1)} %get-tuple-element.865), channel_id=1, source_target_pairs={{0,8},{8,16},{16,24},{24,32},{32,40},{40,48},{48,56},{56,64},{64,7... | collective-permute-start | bytes 589832 | tf_op jit(solution)/shard_map/while/body/eval_jaxpr/ppermute | solution.py:18
  381.3 11.3 %collective-permute-start.4 = (bf16[2,1,64,768]{3,1,2,0:T(2,128)(2,1)S(1)}, bf16[2,1,64,768]{3,1,2,0:T(2,128)(2,1)S(1)}, u32[]{:S(2)}, u32[]{:S(2)}) collective-permute-start(bf16[2,1,64,768]{3,1,2,0:T(2,128)(2,1)S(1)} %get-tuple-element.864), channel_id=1, source_target_pairs={{8,0},{16,8},{24,16},{32,24},{40,32},{48,40},{56,48},{64,56},{72,6... | collective-permute-start | bytes 589832 | tf_op jit(solution)/shard_map/while/body/eval_jaxpr/ppermute | solution.py:19
  382.6 11.5 %collective-permute-start.5 = (bf16[2,1,64,768]{3,1,2,0:T(2,128)(2,1)S(1)}, bf16[2,1,64,768]{3,1,2,0:T(2,128)(2,1)S(1)}, u32[]{:S(2)}, u32[]{:S(2)}) collective-permute-start(bf16[2,1,64,768]{3,1,2,0:T(2,128)(2,1)S(1)} %get-tuple-element.865), channel_id=1, source_target_pairs={{0,8},{8,16},{16,24},{24,32},{32,40},{40,48},{48,56},{56,64},{64,7... | collective-permute-start | bytes 589832 | tf_op jit(solution)/shard_map/while/body/eval_jaxpr/ppermute | solution.py:18
  411.3 12.0 %collective-permute-start.4 = (bf16[2,1,64,768]{3,1,2,0:T(2,128)(2,1)S(1)}, bf16[2,1,64,768]{3,1,2,0:T(2,128)(2,1)S(1)}, u32[]{:S(2)}, u32[]{:S(2)}) collective-permute-start(bf16[2,1,64,768]{3,1,2,0:T(2,128)(2,1)S(1)} %get-tuple-element.864), channel_id=1, source_target_pairs={{8,0},{16,8},{24,16},{32,24},{40,32},{48,40},{56,48},{64,56},{72,6... | collective-permute-start | bytes 589832 | tf_op jit(solution)/shard_map/while/body/eval_jaxpr/ppermute | solution.py:19
  412.6 12.4 %collective-permute-start.5 = (bf16[2,1,64,768]{3,1,2,0:T(2,128)(2,1)S(1)}, bf16[2,1,64,768]{3,1,2,0:T(2,128)(2,1)S(1)}, u32[]{:S(2)}, u32[]{:S(2)}) collective-permute-start(bf16[2,1,64,768]{3,1,2,0:T(2,128)(2,1)S(1)} %get-tuple-element.865), channel_id=1, source_target_pairs={{0,8},{8,16},{16,24},{24,32},{32,40},{40,48},{48,56},{56,64},{64,7... | collective-permute-start | bytes 589832 | tf_op jit(solution)/shard_map/while/body/eval_jaxpr/ppermute | solution.py:18
  457.0 162.8 %collective-permute-start.3 = (bf16[128,768]{1,0:T(8,128)(2,1)S(1)}, bf16[128,768]{1,0:T(8,128)(2,1)S(1)}, u32[]{:S(2)}, u32[]{:S(2)}) collective-permute-start(bf16[128,768]{1,0:T(8,128)(2,1)S(1)} %get-tuple-element.927), channel_id=1, source_target_pairs={{1,0},{2,1},{3,2},{4,3},{5,4},{6,5},{7,6},{9,8},{10,9},{11,10},{12... | collective-permute-start | bytes 589832 | tf_op jit(solution)/shard_map/while/body/eval_jaxpr/ppermute | solution.py:27
  655.8 11.9 %collective-permute-start.4 = (bf16[2,1,64,768]{3,1,2,0:T(2,128)(2,1)S(1)}, bf16[2,1,64,768]{3,1,2,0:T(2,128)(2,1)S(1)}, u32[]{:S(2)}, u32[]{:S(2)}) collective-permute-start(bf16[2,1,64,768]{3,1,2,0:T(2,128)(2,1)S(1)} %get-tuple-element.864), channel_id=1, source_target_pairs={{8,0},{16,8},{24,16},{32,24},{40,32},{48,40},{56,48},{64,56},{72,6... | collective-permute-start | bytes 589832 | tf_op jit(solution)/shard_map/while/body/eval_jaxpr/ppermute | solution.py:19
  657.1 12.4 %collective-permute-start.5 = (bf16[2,1,64,768]{3,1,2,0:T(2,128)(2,1)S(1)}, bf16[2,1,64,768]{3,1,2,0:T(2,128)(2,1)S(1)}, u32[]{:S(2)}, u32[]{:S(2)}) collective-permute-start(bf16[2,1,64,768]{3,1,2,0:T(2,128)(2,1)S(1)} %get-tuple-element.865), channel_id=1, source_target_pairs={{0,8},{8,16},{16,24},{24,32},{32,40},{40,48},{48,56},{56,64},{64,7... | collective-permute-start | bytes 589832 | tf_op jit(solution)/shard_map/while/body/eval_jaxpr/ppermute | solution.py:18
  742.6 13.3 %collective-permute-start.4 = (bf16[2,1,64,768]{3,1,2,0:T(2,128)(2,1)S(1)}, bf16[2,1,64,768]{3,1,2,0:T(2,128)(2,1)S(1)}, u32[]{:S(2)}, u32[]{:S(2)}) collective-permute-start(bf16[2,1,64,768]{3,1,2,0:T(2,128)(2,1)S(1)} %get-tuple-element.864), channel_id=1, source_target_pairs={{8,0},{16,8},{24,16},{32,24},{40,32},{48,40},{56,48},{64,56},{72,6... | collective-permute-start | bytes 589832 | tf_op jit(solution)/shard_map/while/body/eval_jaxpr/ppermute | solution.py:19
  743.9 13.2 %collective-permute-start.5 = (bf16[2,1,64,768]{3,1,2,0:T(2,128)(2,1)S(1)}, bf16[2,1,64,768]{3,1,2,0:T(2,128)(2,1)S(1)}, u32[]{:S(2)}, u32[]{:S(2)}) collective-permute-start(bf16[2,1,64,768]{3,1,2,0:T(2,128)(2,1)S(1)} %get-tuple-element.865), channel_id=1, source_target_pairs={{0,8},{8,16},{16,24},{24,32},{32,40},{40,48},{48,56},{56,64},{64,7... | collective-permute-start | bytes 589832 | tf_op jit(solution)/shard_map/while/body/eval_jaxpr/ppermute | solution.py:18
  761.8 37.6 %collective-permute-start.3 = (bf16[128,768]{1,0:T(8,128)(2,1)S(1)}, bf16[128,768]{1,0:T(8,128)(2,1)S(1)}, u32[]{:S(2)}, u32[]{:S(2)}) collective-permute-start(bf16[128,768]{1,0:T(8,128)(2,1)S(1)} %get-tuple-element.927), channel_id=1, source_target_pairs={{1,0},{2,1},{3,2},{4,3},{5,4},{6,5},{7,6},{9,8},{10,9},{11,10},{12... | collective-permute-start | bytes 589832 | tf_op jit(solution)/shard_map/while/body/eval_jaxpr/ppermute | solution.py:27
  803.2 12.0 %collective-permute-start.4 = (bf16[2,1,64,768]{3,1,2,0:T(2,128)(2,1)S(1)}, bf16[2,1,64,768]{3,1,2,0:T(2,128)(2,1)S(1)}, u32[]{:S(2)}, u32[]{:S(2)}) collective-permute-start(bf16[2,1,64,768]{3,1,2,0:T(2,128)(2,1)S(1)} %get-tuple-element.864), channel_id=1, source_target_pairs={{8,0},{16,8},{24,16},{32,24},{40,32},{48,40},{56,48},{64,56},{72,6... | collective-permute-start | bytes 589832 | tf_op jit(solution)/shard_map/while/body/eval_jaxpr/ppermute | solution.py:19
  (66 other events, 715.3 us)
Sparse Core Ops, SparseCore 0:
  11.2 108.5 all-gather.2
  829.7 282.2 reduce-scatter.3
